TPU v7x, 128 devices: a whole 4x4x4 slice. The times are simulated.
128 devices in a mesh: fsdp: 32 (over x, z, core), tensor: 4 (over y).
Axes of the slice: x: 4, y: 4, z: 4, core: 2. Of those that a mesh axis runs over, the one named last changes fastest.
Arguments:
- tokens: bfloat16 [24576, 8192], P('fsdp'), may hold values from -6 to 6
- weight: bfloat16 [8192, 8192], P('fsdp', 'tensor'), may hold values from -0.0625 to 0.0625
- momentum: float32 [8192, 8192], P('fsdp', 'tensor'), may hold values from -700 to 700
- gradient: bfloat16 [8192, 8192], P('fsdp', 'tensor'), may hold values from -6 to 6
- probes: float32 [32, 8192], P(None, 'tensor'), may hold values from -6 to 6
Outputs:
- activations: float32 [24576, 8192], P('fsdp', 'tensor')
- momentum_out: float32 [8192, 8192], P('fsdp', 'tensor')
- krylov_scaled: float32 [96, 96], replicated
All inputs are finite; a program needn't handle non-finite values.
Results may differ from a plain program's by a relative error of at most 0.0029.
Values may be sent and summed in bfloat16 or wider, within the bound.
A program may use at most 192 MiB of HBM per device.

v0:
```python
import jax
import jax.numpy as jnp
from jax import lax
from jax.sharding import PartitionSpec as P

STEPS = 3
POWER = 32
highest = lax.Precision.HIGHEST
decay_factor = 0.9


def hdot(left, right):
    return jnp.dot(left, right, precision=highest, preferred_element_type=jnp.float32)


def orthonormal(block_mat, gram_mat):
    factor_low = jnp.linalg.cholesky(gram_mat)
    basis_next = jax.scipy.linalg.solve_triangular(factor_low, block_mat, lower=True)
    return (basis_next, factor_low)


def assemble(diag_blocks, low_factors):
    blk_width = diag_blocks[0].shape[0]
    total_size = len(diag_blocks) * blk_width
    krylov = jnp.zeros((total_size, total_size), jnp.float32)
    for position, diag_mat in enumerate(diag_blocks):
        first_at = position * blk_width
        krylov = krylov.at[first_at : first_at + blk_width, first_at : first_at + blk_width].set(
            diag_mat
        )
    for position, factor_low in enumerate(low_factors):
        first_at = position * blk_width
        second_at = first_at + blk_width
        krylov = krylov.at[second_at : second_at + blk_width, first_at:second_at].set(factor_low.T)
        krylov = krylov.at[first_at:second_at, second_at : second_at + blk_width].set(factor_low)
    return krylov


def top_value(krylov):

    def advance(position, vector):
        moved = hdot(krylov, vector)
        return moved / jnp.sqrt(jnp.sum(moved * moved))

    vector = lax.fori_loop(0, POWER, advance, jnp.ones((krylov.shape[0],), jnp.float32))
    return jnp.sum(vector * hdot(krylov, vector))


def local(tokens, weight, momentum, gradient, probes):
    moment = decay_factor * momentum + gradient.astype(jnp.float32)
    num_probes = probes.shape[0]

    def block_sum(values):
        return lax.psum(values, "tensor")

    basis_now, factor_first = orthonormal(probes, block_sum(hdot(probes, probes.T)))
    basis_prev = jnp.zeros_like(basis_now)
    low_prev = jnp.zeros((num_probes, num_probes), jnp.float32)
    diag_blocks = []
    low_factors = []
    for lanczos_step in range(STEPS):
        basis_full = basis_now
        reduced = lax.psum(hdot(basis_full, moment.T), "tensor")
        images = lax.psum(hdot(reduced, moment), "fsdp")
        diag_raw = block_sum(hdot(basis_now, images.T))
        diag_mat = 0.5 * (diag_raw + diag_raw.T)
        diag_blocks.append(diag_mat)
        if lanczos_step + 1 < STEPS:
            residue = images - hdot(diag_mat, basis_now) - hdot(low_prev.T, basis_prev)
            basis_next, factor_low = orthonormal(residue, block_sum(hdot(residue, residue.T)))
            low_factors.append(factor_low)
            basis_prev, low_prev, basis_now = (basis_now, factor_low, basis_next)
    krylov = assemble(diag_blocks, low_factors)
    top = top_value(krylov)
    new_weight = (weight.astype(jnp.float32) - moment / jnp.sqrt(top)).astype(jnp.bfloat16)
    summed = jnp.dot(
        tokens,
        lax.all_gather(new_weight, "fsdp", axis=0, tiled=True),
        preferred_element_type=jnp.float32,
    )
    return (summed, moment, krylov / top)


def solution(mesh):
    return jax.shard_map(
        local,
        mesh=mesh,
        in_specs=(
            P("fsdp", None),
            P("fsdp", "tensor"),
            P("fsdp", "tensor"),
            P("fsdp", "tensor"),
            P(None, "tensor"),
        ),
        out_specs=(P("fsdp", "tensor"), P("fsdp", "tensor"), P()),
        check_vma=False,
    )
```

profile of v0, /device:TPU:1, one launch (start us, length us, event | category | flops | bytes accessed | tf_op | source)
XLA Modules:
  0.0 754.3 jit_solution(2024428877943884364)
XLA Ops:
  8.5 14.2 %psum.84 = f32[32,32]{0,1:T(8,128)S(1)} all-reduce(f32[32,32]{0,1:T(8,128)S(1)} %fusion.24), channel_id=1, replica_groups=mesh['fsdp'=32,'tensor'=4] {'tensor'}, use_global_device_ids=true, to_apply=%region_0.0 | all-reduce | flops 1024 | bytes 8192 | tf_op jit(solution)/shard_map/psum | solution.py:54
  22.8 2.9 cholesky.59
  27.0 2.4 custom-call.8
  29.9 2.3 convert_add_fusion
  34.2 11.1 %psum.85 = f32[32,256]{1,0:T(8,128)S(1)} all-reduce(f32[32,256]{1,0:T(8,128)S(1)} %fusion.25), channel_id=1, replica_groups=mesh['fsdp'=32,'tensor'=4] {'tensor'}, use_global_device_ids=true, to_apply=%region_3.0 | all-reduce | flops 8192 | bytes 65536 | tf_op jit(solution)/shard_map/psum | solution.py:63
  47.4 109.7 %all-reduce.5.cloned.1.call-done = f32[32,2048]{1,0:T(8,128)} async-done(((f32[32,2048]{1,0:T(8,128)}), f32[32,2048]{1,0:T(8,128)}) %all-reduce.5.cloned.1.call-update) | async-done | bytes 262160 | tf_op jit(solution)/shard_map/psum | solution.py:64
  158.4 13.1 %psum.87 = f32[32,32]{0,1:T(8,128)S(1)} all-reduce(f32[32,32]{0,1:T(8,128)S(1)} %fusion.27), channel_id=1, replica_groups=mesh['fsdp'=32,'tensor'=4] {'tensor'}, use_global_device_ids=true, to_apply=%region_5.0 | all-reduce | flops 1024 | bytes 8192 | tf_op jit(solution)/shard_map/psum | solution.py:54
  173.6 11.1 %psum.88 = f32[32,32]{0,1:T(8,128)S(1)} all-reduce(f32[32,32]{0,1:T(8,128)S(1)} %fusion.28), channel_id=1, replica_groups=mesh['fsdp'=32,'tensor'=4] {'tensor'}, use_global_device_ids=true, to_apply=%region_6.0 | all-reduce | flops 1024 | bytes 8192 | tf_op jit(solution)/shard_map/psum | solution.py:54
  184.7 2.9 cholesky.70
  188.9 2.4 custom-call.9
  193.8 11.3 %psum.89 = f32[32,256]{1,0:T(8,128)S(1)} all-reduce(f32[32,256]{1,0:T(8,128)S(1)} %fusion.29), channel_id=1, replica_groups=mesh['fsdp'=32,'tensor'=4] {'tensor'}, use_global_device_ids=true, to_apply=%region_7.0 | all-reduce | flops 8192 | bytes 65536 | tf_op jit(solution)/shard_map/psum | solution.py:63
  207.2 110.4 %all-reduce.7.cloned.1.call-done = f32[32,2048]{1,0:T(8,128)} async-done(((f32[32,2048]{1,0:T(8,128)}), f32[32,2048]{1,0:T(8,128)}) %all-reduce.7.cloned.1.call-update) | async-done | bytes 262160 | tf_op jit(solution)/shard_map/psum | solution.py:64
  318.9 13.1 %psum.91 = f32[32,32]{0,1:T(8,128)S(1)} all-reduce(f32[32,32]{0,1:T(8,128)S(1)} %fusion.31), channel_id=1, replica_groups=mesh['fsdp'=32,'tensor'=4] {'tensor'}, use_global_device_ids=true, to_apply=%region_9.0 | all-reduce | flops 1024 | bytes 8192 | tf_op jit(solution)/shard_map/psum | solution.py:54
  334.2 11.2 %psum.92 = f32[32,32]{0,1:T(8,128)S(1)} all-reduce(f32[32,32]{0,1:T(8,128)S(1)} %fusion.32), channel_id=1, replica_groups=mesh['fsdp'=32,'tensor'=4] {'tensor'}, use_global_device_ids=true, to_apply=%region_10.0 | all-reduce | flops 1024 | bytes 8192 | tf_op jit(solution)/shard_map/psum | solution.py:54
  345.5 2.9 cholesky.81
  349.7 2.4 custom-call.10
  354.5 11.1 %psum.93 = f32[32,256]{1,0:T(8,128)S(1)} all-reduce(f32[32,256]{1,0:T(8,128)S(1)} %fusion.33), channel_id=1, replica_groups=mesh['fsdp'=32,'tensor'=4] {'tensor'}, use_global_device_ids=true, to_apply=%region_11.0 | all-reduce | flops 8192 | bytes 65536 | tf_op jit(solution)/shard_map/psum | solution.py:63
  370.1 108.0 %all-reduce.9.cloned.1.call-done = f32[32,2048]{1,0:T(8,128)} async-done(((f32[32,2048]{1,0:T(8,128)}), f32[32,2048]{1,0:T(8,128)}) %all-reduce.9.cloned.1.call-update) | async-done | bytes 262160 | tf_op jit(solution)/shard_map/psum | solution.py:64
  479.5 13.1 %psum.95 = f32[32,32]{0,1:T(8,128)S(1)} all-reduce(f32[32,32]{0,1:T(8,128)S(1)} %fusion.35), channel_id=1, replica_groups=mesh['fsdp'=32,'tensor'=4] {'tensor'}, use_global_device_ids=true, to_apply=%region_13.0 | all-reduce | flops 1024 | bytes 8192 | tf_op jit(solution)/shard_map/psum | solution.py:54
  496.1 2.1 scatter.30
  500.0 87.1 %while.18 = (s32[]{:T(128)}, f32[96]{0:T(128)}, f32[96,96]{1,0:T(8,128)S(1)}, s32[]{:T(128)}, s32[]{:T(128)}) while((s32[]{:T(128)}, f32[96]{0:T(128)}, f32[96,96]{1,0:T(8,128)S(1)}, s32[]{:T(128)}, s32[]{:T(128)}) %tuple.63), condition=%wide.region_17.0_spmd.clone, body=%wide.region_15.19_spmd.clone.sunk | while | flops 110978 | bytes 38487 | solution.py:45
  592.0 114.0 %all-gather.2.cloned.1.call-done = bf16[8192,2048]{1,0:T(8,128)(2,1)} async-done(((bf16[256,2048]{1,0:T(8,128)(2,1)}), bf16[8192,2048]{1,0:T(8,128)(2,1)}) %all-gather.2.cloned.1.call-update) | async-done | bytes 33554448 | tf_op jit(solution)/shard_map/all_gather | solution.py:78
  705.9 35.2 %convolution_bitcast_fusion.1 = f32[768,2048]{0,1:T(8,128)} fusion(bf16[8192,2048]{1,0:T(8,128)(2,1)} %all-gather.2.cloned.1.call-done, bf16[768,8192]{1,0:T(8,128)(2,1)} %param.24), kind=kOutput, calls=%fused_computation.7 | convolution fusion | flops 25769803776 | bytes 52428800 | tf_op jit(solution)/shard_map/dot_general | solution.py:76
  741.1 6.6 copy.22
  (136 shorter events, 103.4 us)
Async XLA Ops:
  7.2 1.0 copy-start
  7.2 149.9 %all-reduce.5.cloned.1.call-start = ((), (), s32[]{:S(2)}) async-start(), calls=%async_computation | async-start | bytes 524288 | tf_op jit(solution)/shard_map/psum | solution.py:64
  32.2 557.1 %copy-start.2 = (f32[256,2048]{1,0:T(8,128)}, f32[256,2048]{1,0:T(8,128)S(1)}, u32[]{:S(2)}) copy-start(f32[256,2048]{1,0:T(8,128)S(1)} %convert_add_fusion) | copy-start | bytes 6291460
  47.3 270.2 %all-reduce.7.cloned.1.call-start = ((), (), s32[]{:S(2)}) async-start(), calls=%async_computation.1 | async-start | bytes 524288 | tf_op jit(solution)/shard_map/psum | solution.py:64
  207.1 271.1 %all-reduce.9.cloned.1.call-start = ((), (), s32[]{:S(2)}) async-start(), calls=%async_computation.2 | async-start | bytes 524288 | tf_op jit(solution)/shard_map/psum | solution.py:64
  365.7 223.7 %copy-start.3 = (bf16[256,2048]{1,0:T(8,128)(2,1)S(1)}, bf16[256,2048]{1,0:T(8,128)(2,1)}, u32[]{:S(2)}) copy-start(bf16[256,2048]{1,0:T(8,128)(2,1)} %param.25) | copy-start | bytes 3145732
  367.7 338.2 %all-gather.2.cloned.1.call-start = ((), (), s32[]{:S(2)}) async-start(), calls=%async_computation.3 | async-start | bytes 34603008 | tf_op jit(solution)/shard_map/all_gather | solution.py:78
  741.1 6.6 copy-start.1
Sparse Core Ops, SparseCore 0:
  47.5 109.6 all-reduce.4
  207.2 110.2 all-reduce.6
  367.8 110.2 all-reduce.8
  590.8 115.0 all-gather.1
where the time goes:
time: 755 us; the launch traced here: 754 us
  waiting for transfers between devices  442 us (59%)
  blocking collectives  109 us (14%)
  matrix products  104 us (14%)
  other arithmetic  46.2 us (6%)
  loops' own time  22.2 us (3%)
  local copies, waits for them, and re-layouts  14.9 us (2%)
  between operations  14.8 us (2%)
    psum x3, waiting for transfers between devices, local(): images = lax.psum(hdot(reduced, moment), 'fsdp')  328 us
    all_gather x1, waiting for transfers between devices, local(): lax.all_gather(new_weight, 'fsdp', axis=0, tiled=True)  114 us
    psum x6, blocking collectives, block_sum(): return lax.psum(values, 'tensor')  75.9 us
    dot_general x49, matrix products, hdot(): jnp.dot(left, right, precision=highest, preferred_element_type=jnp.float32)  67.9 us
    dot_general x1, matrix products, local(): jnp.dot(tokens, lax.all_gather(new_weight, 'fsdp', axis=0, tiled=True), p...  35.2 us
    psum x3, blocking collectives, local(): reduced = lax.psum(hdot(basis_full, moment.T), 'tensor')  33.5 us
    another operation x1, loops' own time, top_value(): lax.fori_loop(0, POWER, advance, jnp.ones((krylov.shape[0],), jnp.float32))  22.2 us
    div x32, other arithmetic, advance(): return moved / jnp.sqrt(jnp.sum(moved * moved))  18.6 us
  transfers between devices with their start and end apart: 4, of which 4 were waited for; matrix products, arithmetic and copies ran while one was open for 0% of the time, Pallas kernels for 0%

commit v1 on v0

--- a/solution.py
+++ b/solution.py
@@ -75,7 +75,9 @@
     new_weight = (weight.astype(jnp.float32) - moment / jnp.sqrt(top)).astype(jnp.bfloat16)
     summed = jnp.dot(
         tokens,
-        lax.all_gather(new_weight, "fsdp", axis=0, tiled=True),
+        jnp.concatenate(
+            lax.all_to_all(jnp.stack([new_weight] * lax.axis_size("fsdp")), "fsdp", 0, 0), axis=0
+        ),
         preferred_element_type=jnp.float32,
     )
     return (summed, moment, krylov / top)

time: 755 us -> 1210 us (1.60)
  the two profiles are of different devices: /device:TPU:1 before, /device:TPU:36 now
where the time goes in v1:
time: 1210 us
  waiting for transfers between devices  845 us (70%)
  blocking collectives  142 us (12%)
  matrix products  104 us (9%)
  other arithmetic  45.2 us (4%)
  local copies, waits for them, and re-layouts  25.9 us (2%)
  loops' own time  22.2 us (2%)
  between operations  14.8 us (1%)
    all_to_all x1, waiting for transfers between devices, local(): lax.all_to_all(jnp.stack([new_weight] * lax.axis_size('fsdp')), 'fsdp', 0...  548 us
    psum x3, waiting for transfers between devices, local(): images = lax.psum(hdot(reduced, moment), 'fsdp')  297 us
    psum x6, blocking collectives, block_sum(): return lax.psum(values, 'tensor')  96.5 us
    dot_general x49, matrix products, hdot(): jnp.dot(left, right, precision=highest, preferred_element_type=jnp.float32)  67.8 us
    psum x3, blocking collectives, local(): reduced = lax.psum(hdot(basis_full, moment.T), 'tensor')  45.5 us
    dot_general x1, matrix products, local(): jnp.dot(tokens, jnp.concatenate(lax.all_to_all(jnp.stack([new_weight] * l...  35.2 us
  transfers between devices with their start and end apart: 4, of which 4 were waited for; matrix products, arithmetic and copies ran while one was open for 0% of the time, Pallas kernels for 0%

profile of v1, /device:TPU:36, one launch (start us, length us, event | category | flops | bytes accessed | tf_op | source)
XLA Modules:
  0.0 1206.2 jit_solution(8497625098727673682)
XLA Ops:
  8.5 17.2 %psum.84 = f32[32,32]{0,1:T(8,128)S(1)} all-reduce(f32[32,32]{0,1:T(8,128)S(1)} %fusion.24), channel_id=1, replica_groups=mesh['fsdp'=32,'tensor'=4] {'tensor'}, use_global_device_ids=true, to_apply=%region_0.0 | all-reduce | flops 1024 | bytes 8192 | tf_op jit(solution)/shard_map/psum | solution.py:54
  25.7 2.9 cholesky.59
  30.0 2.4 custom-call.8
  37.1 14.4 %psum.85 = f32[32,256]{1,0:T(8,128)S(1)} all-reduce(f32[32,256]{1,0:T(8,128)S(1)} %fusion.25), channel_id=1, replica_groups=mesh['fsdp'=32,'tensor'=4] {'tensor'}, use_global_device_ids=true, to_apply=%region_3.0 | all-reduce | flops 8192 | bytes 65536 | tf_op jit(solution)/shard_map/psum | solution.py:63
  53.6 101.1 %all-reduce.5.cloned.1.call-done = f32[32,2048]{1,0:T(8,128)} async-done(((f32[32,2048]{1,0:T(8,128)}), f32[32,2048]{1,0:T(8,128)}) %all-reduce.5.cloned.1.call-update) | async-done | bytes 262160 | tf_op jit(solution)/shard_map/psum | solution.py:64
  156.0 16.9 %psum.87 = f32[32,32]{0,1:T(8,128)S(1)} all-reduce(f32[32,32]{0,1:T(8,128)S(1)} %fusion.27), channel_id=1, replica_groups=mesh['fsdp'=32,'tensor'=4] {'tensor'}, use_global_device_ids=true, to_apply=%region_5.0 | all-reduce | flops 1024 | bytes 8192 | tf_op jit(solution)/shard_map/psum | solution.py:54
  174.9 14.3 %psum.88 = f32[32,32]{0,1:T(8,128)S(1)} all-reduce(f32[32,32]{0,1:T(8,128)S(1)} %fusion.28), channel_id=1, replica_groups=mesh['fsdp'=32,'tensor'=4] {'tensor'}, use_global_device_ids=true, to_apply=%region_6.0 | all-reduce | flops 1024 | bytes 8192 | tf_op jit(solution)/shard_map/psum | solution.py:54
  189.2 2.9 cholesky.70
  193.5 2.4 custom-call.9
  198.3 15.6 %psum.89 = f32[32,256]{1,0:T(8,128)S(1)} all-reduce(f32[32,256]{1,0:T(8,128)S(1)} %fusion.29), channel_id=1, replica_groups=mesh['fsdp'=32,'tensor'=4] {'tensor'}, use_global_device_ids=true, to_apply=%region_7.0 | all-reduce | flops 8192 | bytes 65536 | tf_op jit(solution)/shard_map/psum | solution.py:63
  216.0 99.1 %all-reduce.7.cloned.1.call-done = f32[32,2048]{1,0:T(8,128)} async-done(((f32[32,2048]{1,0:T(8,128)}), f32[32,2048]{1,0:T(8,128)}) %all-reduce.7.cloned.1.call-update) | async-done | bytes 262160 | tf_op jit(solution)/shard_map/psum | solution.py:64
  316.4 16.9 %psum.91 = f32[32,32]{0,1:T(8,128)S(1)} all-reduce(f32[32,32]{0,1:T(8,128)S(1)} %fusion.31), channel_id=1, replica_groups=mesh['fsdp'=32,'tensor'=4] {'tensor'}, use_global_device_ids=true, to_apply=%region_9.0 | all-reduce | flops 1024 | bytes 8192 | tf_op jit(solution)/shard_map/psum | solution.py:54
  335.5 14.5 %psum.92 = f32[32,32]{0,1:T(8,128)S(1)} all-reduce(f32[32,32]{0,1:T(8,128)S(1)} %fusion.32), channel_id=1, replica_groups=mesh['fsdp'=32,'tensor'=4] {'tensor'}, use_global_device_ids=true, to_apply=%region_10.0 | all-reduce | flops 1024 | bytes 8192 | tf_op jit(solution)/shard_map/psum | solution.py:54
  350.0 2.9 cholesky.81
  354.3 2.4 custom-call.10
  359.1 15.4 %psum.93 = f32[32,256]{1,0:T(8,128)S(1)} all-reduce(f32[32,256]{1,0:T(8,128)S(1)} %fusion.33), channel_id=1, replica_groups=mesh['fsdp'=32,'tensor'=4] {'tensor'}, use_global_device_ids=true, to_apply=%region_11.0 | all-reduce | flops 8192 | bytes 65536 | tf_op jit(solution)/shard_map/psum | solution.py:63
  378.9 96.8 %all-reduce.9.cloned.1.call-done = f32[32,2048]{1,0:T(8,128)} async-done(((f32[32,2048]{1,0:T(8,128)}), f32[32,2048]{1,0:T(8,128)}) %all-reduce.9.cloned.1.call-update) | async-done | bytes 262160 | tf_op jit(solution)/shard_map/psum | solution.py:64
  477.1 16.9 %psum.95 = f32[32,32]{0,1:T(8,128)S(1)} all-reduce(f32[32,32]{0,1:T(8,128)S(1)} %fusion.35), channel_id=1, replica_groups=mesh['fsdp'=32,'tensor'=4] {'tensor'}, use_global_device_ids=true, to_apply=%region_13.0 | all-reduce | flops 1024 | bytes 8192 | tf_op jit(solution)/shard_map/psum | solution.py:54
  501.3 87.1 %while.18 = (s32[]{:T(128)}, f32[96]{0:T(128)}, f32[96,96]{1,0:T(8,128)S(1)}, s32[]{:T(128)}, s32[]{:T(128)}) while((s32[]{:T(128)}, f32[96]{0:T(128)}, f32[96,96]{1,0:T(8,128)S(1)}, s32[]{:T(128)}, s32[]{:T(128)}) %tuple.63), condition=%wide.region_17.0_spmd.clone, body=%wide.region_15.19_spmd.clone.sunk | while | flops 110978 | bytes 38487 | solution.py:45
  590.9 11.0 stack.2
  602.0 7.0 all-to-all-start
  610.2 547.7 %all-to-all-done = bf16[32,256,2048]{2,1,0:T(8,128)(2,1)} async-done(((bf16[32,256,2048]{2,1,0:T(8,128)(2,1)}), bf16[32,256,2048]{2,1,0:T(8,128)(2,1)}, u32[]{:S(2)}, u32[]{:S(2)}) %all-to-all-start) | async-done | bytes 33554464 | tf_op jit(solution)/shard_map/all_to_all | solution.py:79
  1157.9 35.2 %convolution_bitcast_fusion.1 = f32[768,2048]{0,1:T(8,128)} fusion(bf16[8192,2048]{1,0:T(8,128)(2,1)} %bitcast.18, bf16[768,8192]{1,0:T(8,128)(2,1)} %param.24), kind=kOutput, calls=%fused_computation.7 | convolution fusion | flops 25769803776 | bytes 52428800 | tf_op jit(solution)/shard_map/dot_general | solution.py:76
  1193.1 6.6 copy.22
  (136 shorter events, 106.7 us)
Async XLA Ops:
  7.2 1.0 copy-start
  7.2 147.5 %all-reduce.5.cloned.1.call-start = ((), (), s32[]{:S(2)}) async-start(), calls=%async_computation.1 | async-start | bytes 524288 | tf_op jit(solution)/shard_map/psum | solution.py:64
  35.2 555.4 %copy-start.2 = (f32[256,2048]{1,0:T(8,128)}, f32[256,2048]{1,0:T(8,128)S(1)}, u32[]{:S(2)}) copy-start(f32[256,2048]{1,0:T(8,128)S(1)} %convert_add_fusion) | copy-start | bytes 6291460
  53.6 261.5 %all-reduce.7.cloned.1.call-start = ((), (), s32[]{:S(2)}) async-start(), calls=%async_computation.2 | async-start | bytes 524288 | tf_op jit(solution)/shard_map/psum | solution.py:64
  216.0 259.8 %all-reduce.9.cloned.1.call-start = ((), (), s32[]{:S(2)}) async-start(), calls=%async_computation.3 | async-start | bytes 524288 | tf_op jit(solution)/shard_map/psum | solution.py:64
  374.5 216.1 %copy-start.3 = (bf16[256,2048]{1,0:T(8,128)(2,1)S(1)}, bf16[256,2048]{1,0:T(8,128)(2,1)}, u32[]{:S(2)}) copy-start(bf16[256,2048]{1,0:T(8,128)(2,1)} %param.25) | copy-start | bytes 3145732
  602.0 555.9 %all-to-all-start = ((bf16[32,256,2048]{2,1,0:T(8,128)(2,1)}), bf16[32,256,2048]{2,1,0:T(8,128)(2,1)}, u32[]{:S(2)}, u32[]{:S(2)}) async-start(bf16[32,256,2048]{2,1,0:T(8,128)(2,1)} %stack.2), calls=%async_computation | async-start | bytes 67108864 | tf_op jit(solution)/shard_map/all_to_all | solution.py:79
  1193.1 6.6 copy-start.1
Sparse Core Ops, SparseCore 0:
  53.7 100.9 all-reduce.4
  216.1 98.9 all-reduce.6
  376.7 99.0 all-reduce.8
